TPU v7x, 32 devices: a whole 2x2x4 slice. The times are simulated.
32 devices in a mesh: fsdp: 2 (over x), ctx: 4 (over z), tp: 4 (over y, core).
Axes of the slice: x: 2, y: 2, z: 4, core: 2. Of those that a mesh axis runs over, the one named last changes fastest.
Arguments:
- tokens: bfloat16 [4, 1024, 2048], P('fsdp', 'ctx'), may hold values from -36 to 36
- cotangent: bfloat16 [4, 1024, 2048], P('fsdp', 'ctx'), may hold values from -9 to 9
- lengths: int32 [4, 2], P('fsdp'), may hold values from 1 to 768, 1024 in all within a row
- deal: int32 [4, 1024], P('fsdp'), may hold values from 0 to 1023, each once within a row
- att_proj: float32 [3, 2048, 2048], P(None, ('fsdp', 'ctx'), 'tp'), may hold values from -0.125 to 0.125
- attn_out: float32 [2048, 2048], P(('fsdp', 'ctx'), 'tp'), may hold values from -0.75 to 0.75
- ff_proj: float32 [2, 2048, 8192], P(None, ('fsdp', 'ctx'), 'tp'), may hold values from -0.125 to 0.125
- ff_out: float32 [2048, 8192], P(('fsdp', 'ctx'), 'tp'), may hold values from -0.0625 to 0.0625
- att_proj_first: float32 [3, 2048, 2048], P(None, ('fsdp', 'ctx'), 'tp')
- attn_out_first: float32 [2048, 2048], P(('fsdp', 'ctx'), 'tp')
- ff_proj_first: float32 [2, 2048, 8192], P(None, ('fsdp', 'ctx'), 'tp')
- ff_out_first: float32 [2048, 8192], P(('fsdp', 'ctx'), 'tp')
- att_proj_second: float32 [3, 2048, 2048], P(None, ('fsdp', 'ctx'), 'tp'), as said below
- attn_out_second: float32 [2048, 2048], P(('fsdp', 'ctx'), 'tp'), as said below
- ff_proj_second: float32 [2, 2048, 8192], P(None, ('fsdp', 'ctx'), 'tp'), as said below
- ff_out_second: float32 [2048, 8192], P(('fsdp', 'ctx'), 'tp'), as said below
Outputs:
- block_out: bfloat16 [4, 1024, 2048], P('fsdp', 'ctx')
- input_grad: float32 [4, 1024, 2048], P('fsdp', 'ctx')
- grad_norm: float32 [1], replicated
- att_proj_grad: float32 [3, 2048, 2048], P(None, ('fsdp', 'ctx'), 'tp')
- attn_out_grad: float32 [2048, 2048], P(('fsdp', 'ctx'), 'tp')
- ff_proj_grad: float32 [2, 2048, 8192], P(None, ('fsdp', 'ctx'), 'tp')
- ff_out_grad: float32 [2048, 8192], P(('fsdp', 'ctx'), 'tp')
- att_proj_first_new: float32 [3, 2048, 2048], P(None, ('fsdp', 'ctx'), 'tp')
- attn_out_first_new: float32 [2048, 2048], P(('fsdp', 'ctx'), 'tp')
- ff_proj_first_new: float32 [2, 2048, 8192], P(None, ('fsdp', 'ctx'), 'tp')
- ff_out_first_new: float32 [2048, 8192], P(('fsdp', 'ctx'), 'tp')
- att_proj_second_new: float32 [3, 2048, 2048], P(None, ('fsdp', 'ctx'), 'tp')
- attn_out_second_new: float32 [2048, 2048], P(('fsdp', 'ctx'), 'tp')
- ff_proj_second_new: float32 [2, 2048, 8192], P(None, ('fsdp', 'ctx'), 'tp')
- ff_out_second_new: float32 [2048, 8192], P(('fsdp', 'ctx'), 'tp')
- att_proj_new: float32 [3, 2048, 2048], P(None, ('fsdp', 'ctx'), 'tp')
- attn_out_new: float32 [2048, 2048], P(('fsdp', 'ctx'), 'tp')
- ff_proj_new: float32 [2, 2048, 8192], P(None, ('fsdp', 'ctx'), 'tp')
- ff_out_new: float32 [2048, 8192], P(('fsdp', 'ctx'), 'tp')
- att_proj_low: bfloat16 [3, 2048, 2048], P(None, ('fsdp', 'ctx'), 'tp')
- attn_out_low: bfloat16 [2048, 2048], P(('fsdp', 'ctx'), 'tp')
- ff_proj_low: bfloat16 [2, 2048, 8192], P(None, ('fsdp', 'ctx'), 'tp')
- ff_out_low: bfloat16 [2048, 8192], P(('fsdp', 'ctx'), 'tp')
Inputs may be any that keep to these rules, and one draw needn't show every extreme that they name: `lengths`: each row sums to 1024 and no entry exceeds 768. `deal`: each row is a permutation of the positions of its pack. `att_proj_second`: every entry is positive. `attn_out_second`: every entry is positive. `ff_proj_second`: every entry is positive. `ff_out_second`: every entry is positive.
All inputs are finite; a program needn't handle non-finite values.
Results may differ from a plain program's by a relative error of at most 0.017.
Values may be sent and summed in bfloat16 or wider, within the bound.
A program may use at most 320 MiB of HBM per device.

v0:
```python
import jax
import jax.numpy as jnp
from jax import lax
from jax.sharding import PartitionSpec as P

HEAD_DIM = 128
STEP = 10
EPS_NORM = 1e-05
BETA_ONE = 0.9
BETA_TWO = 0.95
EPS_ADAM = 1e-08
DECAY = 0.1
MAX_NORM = 1.0
NEG_FILL = -1e30
BF = jnp.bfloat16
F32 = jnp.float32


def mean_spread(values):
    centre = values - jnp.mean(values, axis=-1, keepdims=True)
    spread = jnp.mean(centre * centre, axis=-1, keepdims=True)
    scale = lax.rsqrt(spread + EPS_NORM)
    return (centre * scale, scale)


def norm_back(grad, normed, scale):
    return scale * (
        grad
        - jnp.mean(grad, axis=-1, keepdims=True)
        - normed * jnp.mean(grad * normed, axis=-1, keepdims=True)
    )


def dot(left, right, dims):
    return lax.dot_general(left, right, (dims, ((), ())), preferred_element_type=F32)


def adam_step(weight, grad_sum, first, second, clip_factor, learn_rate):
    clipped = grad_sum * clip_factor
    first_new = BETA_ONE * first + (1.0 - BETA_ONE) * clipped
    second_new = BETA_TWO * second + (1.0 - BETA_TWO) * clipped * clipped
    first_hat = first_new / (1.0 - BETA_ONE**STEP)
    second_hat = second_new / (1.0 - BETA_TWO**STEP)
    weight_new = weight - learn_rate * (
        first_hat / (jnp.sqrt(second_hat) + EPS_ADAM) + DECAY * weight
    )
    return (first_new, second_new, weight_new)


def make_shards(mesh):
    n_f, n_c, n_t = (mesh.shape[a] for a in ("fsdp", "ctx", "tp"))

    def by_ctx(block, shift):
        return lax.ppermute(block, "ctx", [(i, (i + shift) % n_c) for i in range(n_c)])

    def by_core(block):
        return lax.ppermute(block, "tp", [(i, i ^ 1) for i in range(n_t)])

    def by_pack(block, shift, other):
        pairs = [
            (f * n_t + t, (f + shift) % n_f * n_t + (t ^ 2 * other))
            for f in range(n_f)
            for t in range(n_t)
        ]
        return lax.ppermute(block, ("fsdp", "tp"), pairs)

    def gather_rows(half):
        mine = jnp.stack([half] + [by_ctx(half, s) for s in range(1, n_c)])
        both = jnp.stack([mine, by_core(mine)], axis=1)
        return both.reshape(-1, half.shape[1])

    def scatter_rows(partial):
        width = partial.shape[1]
        split = partial.astype(BF).reshape(n_c, 2, -1, width)
        summed = split[:, 0].astype(F32) + by_core(split[:, 1]).astype(F32)
        sent = summed.astype(BF)
        total = summed[0]
        for j in range(1, n_c):
            total = total + by_ctx(sent[j], -j).astype(F32)
        return total

    def gather_weight(shard):
        swapped = lax.all_to_all(shard.astype(BF), "ctx", 2, 1, tiled=True)
        columns = []
        for other in range(2):
            parts = [
                swapped if s == 0 and other == 0 else by_pack(swapped, s, other) for s in range(n_f)
            ]
            columns.append(jnp.concatenate(parts, axis=1))
        return jnp.concatenate(columns, axis=2)

    def scatter_grad(grad):
        count, height, width = grad.shape
        low = grad.astype(BF).reshape(count, n_f, height // n_f, 2, width // 2)
        total = grad.reshape(low.shape)[:, 0, :, 0]
        for other in range(2):
            for i in range(n_f):
                if i or other:
                    total = total + by_pack(low[:, i, :, other], -i, other).astype(F32)
        return lax.all_to_all(total.astype(BF), "ctx", 1, 2, tiled=True).astype(F32)

    def shards(
        tokens,
        cotangent,
        lengths,
        deal,
        att_proj,
        attn_out,
        ff_proj,
        ff_out,
        att_proj_first,
        attn_out_first,
        ff_proj_first,
        ff_out_first,
        att_proj_second,
        attn_out_second,
        ff_proj_second,
        ff_out_second,
    ):
        f_at, c_at, t_at = (lax.axis_index(a) for a in ("fsdp", "ctx", "tp"))
        pack_at, core_at = (t_at // 2, t_at % 2)
        packs, row_count, width = tokens.shape
        half = row_count // 2
        pack_len = deal.shape[1]
        score_scale = HEAD_DIM ** (-0.5)
        f_width = width // n_f

        def turned(rows):
            return jnp.concatenate(
                [
                    lax.dynamic_slice_in_dim(rows, (f_at - i) % n_f * f_width, f_width, 1)
                    for i in range(n_f)
                ],
                axis=1,
            )

        def own_rows(array):
            rows = array.reshape(packs * 2, half, width)
            return turned(lax.dynamic_index_in_dim(rows, t_at, 0, keepdims=False))

        own_tokens = own_rows(tokens)
        own_cot = own_rows(cotangent)
        att_w = gather_weight(jnp.concatenate([att_proj, attn_out[None]]))
        own_input = own_tokens.astype(F32)
        normed_one, scale_one = mean_spread(own_input)
        act_one = gather_rows(normed_one.astype(BF))
        deal_pack = lax.dynamic_index_in_dim(deal, pack_at, 0, keepdims=False)
        length_row = lax.dynamic_index_in_dim(lengths, pack_at, 0, keepdims=False)
        places = jnp.concatenate(
            [
                lax.dynamic_slice_in_dim(
                    deal_pack, (c_at - j) % n_c * row_count + (core_at + h) % 2 * half, half
                )
                for j in range(n_c)
                for h in range(2)
            ]
        )
        seqs = lengths.shape[1]
        before = jnp.arange(seqs)[:, None] > jnp.arange(seqs)[None, :]
        starts = jnp.sum(jnp.where(before, length_row[None, :], 0), axis=1)
        inside = (places[:, None] >= starts[None, :]) & (
            places[:, None] < (starts + length_row)[None, :]
        )
        firsts = jnp.sum(jnp.where(inside, starts[None, :], 0), axis=1)
        allowed = (places[None, :] <= places[:, None]) & (places[None, :] >= firsts[:, None])
        freq_steps = jnp.arange(HEAD_DIM // 2, dtype=F32)
        inverse = jnp.power(10000.0, -2.0 * freq_steps / HEAD_DIM)
        angles = (places - firsts).astype(F32)[:, None] * inverse[None, :]
        cos_table, sine_table = (jnp.cos(angles), jnp.sin(angles))

        def turn(values, sign):
            low, high = (values[..., : HEAD_DIM // 2], values[..., HEAD_DIM // 2 :])
            sine = sign * sine_table[:, None, :]
            cos = cos_table[:, None, :]
            return jnp.concatenate([low * cos - high * sine, high * cos + low * sine], axis=-1)

        rank_width = att_w.shape[2]
        heads = rank_width // HEAD_DIM
        raw = [
            dot(act_one, att_w[i], ((1,), (0,))).reshape(pack_len, heads, HEAD_DIM)
            for i in range(3)
        ]
        query = turn(raw[0], 1.0).astype(BF)
        key = turn(raw[1], 1.0).astype(BF)
        value = raw[2].astype(BF)
        scores = jnp.einsum("thd,khd->htk", query, key, preferred_element_type=F32) * score_scale
        scores = jnp.where(allowed[None], scores, NEG_FILL)
        exp_scores = jnp.exp(scores - jnp.max(scores, axis=2, keepdims=True))
        probs = exp_scores / jnp.sum(exp_scores, axis=2, keepdims=True)
        probs_low = probs.astype(BF)
        attended = jnp.einsum("htk,khd->thd", probs_low, value, preferred_element_type=F32)
        attended_low = attended.reshape(pack_len, rank_width).astype(BF)
        out_part = dot(attended_low, att_w[3], ((1,), (1,)))
        resid_mid = own_input + scatter_rows(out_part)
        normed_two, scale_two = mean_spread(resid_mid)
        act_two = gather_rows(normed_two.astype(BF))
        ff_w = gather_weight(jnp.concatenate([ff_proj, ff_out[None]]))
        cot_rows = gather_rows(own_cot)
        up = dot(act_two, ff_w[0], ((1,), (0,)))
        gate = dot(act_two, ff_w[1], ((1,), (0,)))
        sigma = jax.nn.sigmoid(gate)
        hidden_low = (gate * sigma * up).astype(BF)
        hidden_grad = dot(cot_rows, ff_w[2], ((1,), (0,)))
        up_grad = (hidden_grad * gate * sigma).astype(BF)
        gate_grad = (hidden_grad * up * sigma * (1.0 + gate * (1.0 - sigma))).astype(BF)
        act_two_part = dot(up_grad, ff_w[0], ((1,), (1,))) + dot(gate_grad, ff_w[1], ((1,), (1,)))
        act_two_grad = scatter_rows(act_two_part)
        mid_grad = own_cot.astype(F32) + norm_back(act_two_grad, normed_two, scale_two)
        mid_rows = gather_rows(mid_grad.astype(BF))
        ff_branch = scatter_rows(dot(hidden_low, ff_w[2], ((1,), (1,))))
        block_rows = turned((resid_mid + ff_branch).astype(BF))
        block_out = lax.all_gather(block_rows, "tp", axis=0, tiled=True)
        ff_grad = jnp.stack(
            [
                dot(act_two, up_grad, ((0,), (0,))),
                dot(act_two, gate_grad, ((0,), (0,))),
                dot(cot_rows, hidden_low, ((0,), (0,))),
            ]
        )
        ff_total = scatter_grad(ff_grad)
        attended_grad = dot(mid_rows, att_w[3], ((1,), (0,))).astype(BF)
        attended_grad = attended_grad.reshape(pack_len, heads, HEAD_DIM)
        value_grad = jnp.einsum(
            "htk,thd->khd", probs_low, attended_grad, preferred_element_type=F32
        )
        prob_grad = jnp.einsum("thd,khd->htk", attended_grad, value, preferred_element_type=F32)
        delta_rows = jnp.sum(probs * prob_grad, axis=2, keepdims=True)
        score_grad = (probs * (prob_grad - delta_rows)).astype(BF)
        query_grad = (
            jnp.einsum("htk,khd->thd", score_grad, key, preferred_element_type=F32) * score_scale
        )
        key_grad = (
            jnp.einsum("htk,thd->khd", score_grad, query, preferred_element_type=F32) * score_scale
        )
        joint_grad = [
            part.reshape(pack_len, rank_width).astype(BF)
            for part in (turn(query_grad, -1.0), turn(key_grad, -1.0), value_grad)
        ]
        act_one_part = sum((dot(joint_grad[i], att_w[i], ((1,), (1,))) for i in range(3)))
        act_one_grad = scatter_rows(act_one_part)
        input_rows = turned(norm_back(act_one_grad, normed_one, scale_one) + mid_grad)
        input_grad = lax.all_gather(input_rows, "tp", axis=0, tiled=True)
        att_grad = jnp.stack(
            [dot(act_one, part, ((0,), (0,))) for part in joint_grad]
            + [dot(mid_rows, attended_low, ((0,), (0,)))]
        )
        att_total = scatter_grad(att_grad)
        square_sum = lax.psum(
            jnp.sum(att_total * att_total) + jnp.sum(ff_total * ff_total), ("fsdp", "ctx", "tp")
        )
        norm_value = jnp.sqrt(square_sum)
        clip_factor = jnp.minimum(1.0, MAX_NORM / (norm_value + 1e-06))
        base_rate = width ** (-0.5)
        out_rate = (width // 32) ** (-0.5)
        grads = (att_total[:3], att_total[3], ff_total[:2], ff_total[2])
        weights = (att_proj, attn_out, ff_proj, ff_out)
        firsts_old = (att_proj_first, attn_out_first, ff_proj_first, ff_out_first)
        seconds_old = (att_proj_second, attn_out_second, ff_proj_second, ff_out_second)
        rates = (base_rate, out_rate, base_rate, base_rate)
        news = [
            adam_step(w, g, m, v, clip_factor, r)
            for w, g, m, v, r in zip(weights, grads, firsts_old, seconds_old, rates)
        ]
        return (
            block_out.reshape(tokens.shape),
            input_grad.reshape(tokens.shape),
            norm_value.reshape(1),
            *grads,
            *(n[0] for n in news),
            *(n[1] for n in news),
            *(n[2] for n in news),
            *(n[2].astype(BF) for n in news),
        )

    return shards


def solution(mesh):
    act = P("fsdp", "ctx", None)
    table = P("fsdp", None)
    cube = P(None, ("fsdp", "ctx"), "tp")
    flat = P(("fsdp", "ctx"), "tp")
    group = (cube, flat, cube, flat)
    in_specs = (act, act, table, table) + group * 3
    out_specs = (act, act, P()) + group * 5
    return jax.shard_map(
        make_shards(mesh), mesh=mesh, in_specs=in_specs, out_specs=out_specs, check_vma=False
    )
```

profile of v0, /device:TPU:0, one launch (start us, length us, event | category | flops | bytes accessed | tf_op | source)
XLA Modules:
  0.0 1239.6 jit_solution(7783477940593059198)
XLA Ops:
  28.0 44.8 %collective-permute-done.1 = bf16[128,2048]{1,0:T(8,128)(2,1)} collective-permute-done((bf16[128,2048]{1,0:T(8,128)(2,1)}, bf16[128,2048]{1,0:T(8,128)(2,1)}, u32[]{:S(2)}, u32[]{:S(2)}) %collective-permute-start.1) | collective-permute-done | bytes 524320 | tf_op jit(solution)/shard_map/ppermute | solution.py:54
  93.8 17.7 %collective-permute-done.6 = bf16[4,1024,128]{1,2,0:T(8,128)(2,1)S(1)} collective-permute-done((bf16[4,1024,128]{1,2,0:T(8,128)(2,1)S(1)}, bf16[4,1024,128]{1,2,0:T(8,128)(2,1)S(1)}, u32[]{:S(2)}, u32[]{:S(2)}) %collective-permute-start.6) | collective-permute-done | bytes 1048608 | tf_op jit(solution)/shard_map/ppermute | solution.py:65
  111.4 20.4 %collective-permute-done.5 = bf16[4,1024,128]{1,2,0:T(8,128)(2,1)S(1)} collective-permute-done((bf16[4,1024,128]{1,2,0:T(8,128)(2,1)S(1)}, bf16[4,1024,128]{1,2,0:T(8,128)(2,1)S(1)}, u32[]{:S(2)}, u32[]{:S(2)}) %collective-permute-start.5) | collective-permute-done | bytes 1048608 | tf_op jit(solution)/shard_map/ppermute | solution.py:65
  189.7 71.6 %collective-permute-done.10 = bf16[128,2048]{1,0:T(8,128)(2,1)S(1)} collective-permute-done((bf16[128,2048]{1,0:T(8,128)(2,1)S(1)}, bf16[128,2048]{1,0:T(8,128)(2,1)S(1)}, u32[]{:S(2)}, u32[]{:S(2)}) %collective-permute-start.10) | collective-permute-done | bytes 524320 | tf_op jit(solution)/shard_map/ppermute | solution.py:54
  261.3 65.1 %collective-permute-start.22 = (bf16[128,2048]{1,0:T(8,128)(2,1)S(1)}, bf16[128,2048]{1,0:T(8,128)(2,1)S(1)}, u32[]{:S(2)}, u32[]{:S(2)}) collective-permute-start(bf16[128,2048]{1,0:T(8,128)(2,1)S(1)} %get-tuple-element.108), channel_id=1, source_target_pairs={{0,4},{4,8},{8,12},{12,0},{1,5},{5,9},{9,13},{13,1},{2,6},{6,10},{... | collective-permute-start | bytes 1572872 | tf_op jit(solution)/shard_map/ppermute | solution.py:54
  329.5 12.8 %collective-permute-start.13 = (bf16[128,2048]{1,0:T(8,128)(2,1)}, bf16[128,2048]{1,0:T(8,128)(2,1)}, u32[]{:S(2)}, u32[]{:S(2)}) collective-permute-start(bf16[128,2048]{1,0:T(8,128)(2,1)} %fusion.76), channel_id=1, source_target_pairs={{0,12},{4,0},{8,4},{12,8},{1,13},{5,1},{9,5},{13,9},{2,14},{6,2},{... | collective-permute-start | bytes 1572872 | tf_op jit(solution)/shard_map/ppermute | solution.py:54
  342.8 8.0 collective-permute-start.11
  350.8 33.1 %collective-permute-done.23 = bf16[128,2048]{1,0:T(8,128)(2,1)S(1)} collective-permute-done((bf16[128,2048]{1,0:T(8,128)(2,1)S(1)}, bf16[128,2048]{1,0:T(8,128)(2,1)S(1)}, u32[]{:S(2)}, u32[]{:S(2)}) %collective-permute-start.23) | collective-permute-done | bytes 524320 | tf_op jit(solution)/shard_map/ppermute | solution.py:54
  397.7 8.1 collective-permute-done.12
  415.5 7.8 reshape.558
  423.3 11.2 copy.390
  451.4 15.5 %collective-permute-done.17 = bf16[3,1024,512]{2,1,0:T(8,128)(2,1)} collective-permute-done((bf16[3,1024,512]{2,1,0:T(8,128)(2,1)}, bf16[3,1024,512]{2,1,0:T(8,128)(2,1)}, u32[]{:S(2)}, u32[]{:S(2)}) %collective-permute-start.17) | collective-permute-done | bytes 3145760 | tf_op jit(solution)/shard_map/ppermute | solution.py:65
  466.9 67.0 %collective-permute-done.16 = bf16[3,1024,512]{2,1,0:T(8,128)(2,1)} collective-permute-done((bf16[3,1024,512]{2,1,0:T(8,128)(2,1)}, bf16[3,1024,512]{2,1,0:T(8,128)(2,1)}, u32[]{:S(2)}, u32[]{:S(2)}) %collective-permute-start.16) | collective-permute-done | bytes 3145760 | tf_op jit(solution)/shard_map/ppermute | solution.py:65
  533.8 14.6 %maximum_maximum_fusion = bf16[3,2048,1024]{2,1,0:T(8,128)(2,1)S(1)} fusion(bf16[3,1024,512]{2,1,0:T(8,128)(2,1)} %collective-permute-done.17, bf16[3,1024,512]{2,1,0:T(8,128)(2,1)} %collective-permute-done.16, bf16[3,1024,512]{2,1,0:T(8,128)(2,1)} %collective-permute-done.15, bf16[3,1024,512]{2,1,0:T(8,128)(2,1)} %bitcast.502), kind=kLoop, calls=%fused_computation.2 | loop fusion | flops 50331648 | bytes 25165824 | tf_op jit(solution)/shard_map/concatenate | solution.py:90
  566.9 14.0 %fusion.12 = (bf16[1024,1024]{1,0:T(8,128)(2,1)}, bf16[1024,1024]{1,0:T(8,128)(2,1)}, bf16[1024,1024]{1,0:T(8,128)(2,1)}, f32[1024,1024]{0,1:T(8,128)}) fusion(f32[1024,1024]{0,1:T(8,128)} %fusion.23, f32[1024,1024]{0,1:T(8,128)} %fusion.22, bf16[1024,2048]{1,0:T(8,128)(2,1)} %bitcast.482, bf16[3,2048,1024]{2,1,0:T(8,128)(2,1)} %copy-done.14), kind=kOutput, calls=%fused_computation.43 | convolution fusion | flops 4311744512 | bytes 27262976 | tf_op jit(solution)/shard_map/dot_general | solution.py:35
  591.7 9.3 convolution_convert_fusion.1
  601.0 10.3 fusion.20
  611.3 11.6 add_convert_fusion.1
  649.8 10.0 collective-permute-done.29
  659.7 22.3 %collective-permute-done.28 = bf16[128,2048]{1,0:T(8,128)(2,1)} collective-permute-done((bf16[128,2048]{1,0:T(8,128)(2,1)}, bf16[128,2048]{1,0:T(8,128)(2,1)}, u32[]{:S(2)}, u32[]{:S(2)}) %collective-permute-start.28) | collective-permute-done | bytes 524320 | tf_op jit(solution)/shard_map/ppermute | solution.py:54
  683.9 9.5 collective-permute-done.21
  693.4 32.7 %collective-permute-done.20 = bf16[128,2048]{1,0:T(8,128)(2,1)S(1)} collective-permute-done((bf16[128,2048]{1,0:T(8,128)(2,1)S(1)}, bf16[128,2048]{1,0:T(8,128)(2,1)S(1)}, u32[]{:S(2)}, u32[]{:S(2)}) %collective-permute-start.20) | collective-permute-done | bytes 524320 | tf_op jit(solution)/shard_map/ppermute | solution.py:54
  726.9 11.0 collective-permute-start.32
  750.4 33.8 %collective-permute-done.31 = bf16[128,2048]{1,0:T(8,128)(2,1)S(1)} collective-permute-done((bf16[128,2048]{1,0:T(8,128)(2,1)S(1)}, bf16[128,2048]{1,0:T(8,128)(2,1)S(1)}, u32[]{:S(2)}, u32[]{:S(2)}) %collective-permute-start.31) | collective-permute-done | bytes 524320 | tf_op jit(solution)/shard_map/ppermute | solution.py:54
  799.4 12.5 %pad_maximum_fusion = f32[3,2,1024,2,512]{4,2,3,1,0:T(8,128)} fusion(f32[1,2,1024,2,512]{4,2,3,1,0:T(8,128)} %convolution_bitcast_fusion, f32[1,2,1024,2,512]{4,2,3,1,0:T(8,128)S(1)} %convolution_bitcast_fusion.1, f32[1,2,1024,2,512]{4,2,3,1,0:T(8,128)S(1)} %convolution_bitcast_fusion.2), kind=kLoop, calls=%fused_computation.1 | loop fusion | flops 12582912 | bytes 50331648 | tf_op jit(solution)/shard_map/stack | solution.py:213
  845.0 23.0 %collective-permute-done.43 = bf16[3,1024,512]{2,1,0:T(8,128)(2,1)} collective-permute-done((bf16[3,1024,512]{2,1,0:T(8,128)(2,1)}, bf16[3,1024,512]{2,1,0:T(8,128)(2,1)}, u32[]{:S(2)}, u32[]{:S(2)}) %collective-permute-start.43) | collective-permute-done | bytes 3145760 | tf_op jit(solution)/shard_map/ppermute | solution.py:65
  868.1 78.2 %collective-permute-done.42 = bf16[3,1024,512]{2,1,0:T(8,128)(2,1)} collective-permute-done((bf16[3,1024,512]{2,1,0:T(8,128)(2,1)}, bf16[3,1024,512]{2,1,0:T(8,128)(2,1)}, u32[]{:S(2)}, u32[]{:S(2)}) %collective-permute-start.42) | collective-permute-done | bytes 3145760 | tf_op jit(solution)/shard_map/ppermute | solution.py:65
  946.3 7.2 fusion.5
  994.9 52.5 %collective-permute-done.37 = bf16[128,2048]{1,0:T(8,128)(2,1)S(1)} collective-permute-done((bf16[128,2048]{1,0:T(8,128)(2,1)S(1)}, bf16[128,2048]{1,0:T(8,128)(2,1)S(1)}, u32[]{:S(2)}, u32[]{:S(2)}) %collective-permute-start.37) | collective-permute-done | bytes 524320 | tf_op jit(solution)/shard_map/ppermute | solution.py:54
  1048.9 42.4 %collective-permute-done.36 = bf16[128,2048]{1,0:T(8,128)(2,1)S(1)} collective-permute-done((bf16[128,2048]{1,0:T(8,128)(2,1)S(1)}, bf16[128,2048]{1,0:T(8,128)(2,1)S(1)}, u32[]{:S(2)}, u32[]{:S(2)}) %collective-permute-start.36) | collective-permute-done | bytes 524320 | tf_op jit(solution)/shard_map/ppermute | solution.py:54
  1100.9 20.4 %all-to-all-start.2 = ((bf16[4,1024,128]{2,0,1:T(4,128)(2,1)}), bf16[4,1024,128]{2,0,1:T(4,128)(2,1)S(1)}, u32[]{:S(2)}, u32[]{:S(2)}) async-start(bf16[4,1024,128]{2,0,1:T(4,128)(2,1)} %copy.371), calls=%async_computation.2 | async-start | bytes 2097152 | tf_op jit(solution)/shard_map/all_to_all | solution.py:100
  1158.8 40.1 %psum.7 = f32[]{:T(128)} all-reduce(f32[]{:T(128)S(6)} %add.425), channel_id=1, replica_groups=mesh['fsdp'=2,'ctx'=4,'tp'=4] {'fsdp','ctx','tp'}, use_global_device_ids=true, to_apply=%region_15.16 | all-reduce | flops 1 | bytes 8 | tf_op jit(solution)/shard_map/psum | solution.py:248
  (382 shorter events, 382.1 us)
Async XLA Ops:
  15.3 57.5 %collective-permute-start.1 = (bf16[128,2048]{1,0:T(8,128)(2,1)}, bf16[128,2048]{1,0:T(8,128)(2,1)}, u32[]{:S(2)}, u32[]{:S(2)}) collective-permute-start(bf16[128,2048]{1,0:T(8,128)(2,1)} %fusion.49), channel_id=1, source_target_pairs={{0,8},{4,12},{8,0},{12,4},{1,9},{5,13},{9,1},{13,5},{2,10},{6,14},... | collective-permute-start | bytes 1572872 | tf_op jit(solution)/shard_map/ppermute | solution.py:54
  15.3 57.5 %collective-permute-start = (bf16[128,2048]{1,0:T(8,128)(2,1)}, bf16[128,2048]{1,0:T(8,128)(2,1)}, u32[]{:S(2)}, u32[]{:S(2)}) collective-permute-start(bf16[128,2048]{1,0:T(8,128)(2,1)} %fusion.49), channel_id=1, source_target_pairs={{0,4},{4,8},{8,12},{12,0},{1,5},{5,9},{9,13},{13,1},{2,6},{6,10},{... | collective-permute-start | bytes 1572872 | tf_op jit(solution)/shard_map/ppermute | solution.py:54
  19.0 63.7 %all-to-all-start = ((bf16[4,256,512]{1,0,2:T(4,128)(2,1)}), bf16[4,256,512]{1,0,2:T(4,128)(2,1)S(1)}, u32[]{:S(2)}, u32[]{:S(2)}) async-start(bf16[4,256,512]{1,0,2:T(4,128)(2,1)} %copy.331), calls=%async_computation | async-start | bytes 2097152 | tf_op jit(solution)/shard_map/all_to_all | solution.py:83
  171.8 213.8 %all-to-all-start.1 = ((bf16[3,256,2048]{1,0,2:T(4,128)(2,1)}), bf16[3,256,2048]{1,0,2:T(4,128)(2,1)}, u32[]{:S(2)}, u32[]{:S(2)}) async-start(bf16[3,256,2048]{1,0,2:T(4,128)(2,1)} %pad_maximum_fusion.4), calls=%async_computation.1 | async-start | bytes 8388608 | tf_op jit(solution)/shard_map/all_to_all | solution.py:83
  177.0 944.3 %all-gather.3.cloned.1.call-start = ((), (), s32[]{:S(2)}) async-start(), calls=%async_computation.4 | async-start | bytes 2621440 | tf_op jit(solution)/shard_map/all_gather | solution.py:212
  180.3 81.0 %collective-permute-start.10 = (bf16[128,2048]{1,0:T(8,128)(2,1)S(1)}, bf16[128,2048]{1,0:T(8,128)(2,1)S(1)}, u32[]{:S(2)}, u32[]{:S(2)}) collective-permute-start(bf16[128,2048]{1,0:T(8,128)(2,1)S(1)} %get-tuple-element.88), channel_id=1, source_target_pairs={{0,4},{4,8},{8,12},{12,0},{1,5},{5,9},{9,13},{13,1},{2,6},{6,10},{... | collective-permute-start | bytes 1572872 | tf_op jit(solution)/shard_map/ppermute | solution.py:54
  182.4 145.3 %collective-permute-start.9 = (bf16[128,2048]{1,0:T(8,128)(2,1)S(1)}, bf16[128,2048]{1,0:T(8,128)(2,1)S(1)}, u32[]{:S(2)}, u32[]{:S(2)}) collective-permute-start(bf16[128,2048]{1,0:T(8,128)(2,1)S(1)} %get-tuple-element.89), channel_id=1, source_target_pairs={{0,8},{4,12},{8,0},{12,4},{1,9},{5,13},{9,1},{13,5},{2,10},{6,14},... | collective-permute-start | bytes 1572872 | tf_op jit(solution)/shard_map/ppermute | solution.py:54
  184.8 143.0 %collective-permute-start.8 = (bf16[128,2048]{1,0:T(8,128)(2,1)S(1)}, bf16[128,2048]{1,0:T(8,128)(2,1)S(1)}, u32[]{:S(2)}, u32[]{:S(2)}) collective-permute-start(bf16[128,2048]{1,0:T(8,128)(2,1)S(1)} %get-tuple-element.87), channel_id=1, source_target_pairs={{0,12},{4,0},{8,4},{12,8},{1,13},{5,1},{9,5},{13,9},{2,14},{6,2},{... | collective-permute-start | bytes 1572872 | tf_op jit(solution)/shard_map/ppermute | solution.py:54
  187.6 155.2 %collective-permute-start.24 = (bf16[128,2048]{1,0:T(8,128)(2,1)S(1)}, bf16[128,2048]{1,0:T(8,128)(2,1)S(1)}, u32[]{:S(2)}, u32[]{:S(2)}) collective-permute-start(bf16[128,2048]{1,0:T(8,128)(2,1)S(1)} %get-tuple-element.108), channel_id=1, source_target_pairs={{0,12},{4,0},{8,4},{12,8},{1,13},{5,1},{9,5},{13,9},{2,14},{6,2},{... | collective-permute-start | bytes 1572872 | tf_op jit(solution)/shard_map/ppermute | solution.py:54
  188.2 195.7 %collective-permute-start.23 = (bf16[128,2048]{1,0:T(8,128)(2,1)S(1)}, bf16[128,2048]{1,0:T(8,128)(2,1)S(1)}, u32[]{:S(2)}, u32[]{:S(2)}) collective-permute-start(bf16[128,2048]{1,0:T(8,128)(2,1)S(1)} %get-tuple-element.108), channel_id=1, source_target_pairs={{0,8},{4,12},{8,0},{12,4},{1,9},{5,13},{9,1},{13,5},{2,10},{6,14},... | collective-permute-start | bytes 1572872 | tf_op jit(solution)/shard_map/ppermute | solution.py:54
  261.3 122.6 %collective-permute-start.22 = (bf16[128,2048]{1,0:T(8,128)(2,1)S(1)}, bf16[128,2048]{1,0:T(8,128)(2,1)S(1)}, u32[]{:S(2)}, u32[]{:S(2)}) collective-permute-start(bf16[128,2048]{1,0:T(8,128)(2,1)S(1)} %get-tuple-element.108), channel_id=1, source_target_pairs={{0,4},{4,8},{8,12},{12,0},{1,5},{5,9},{9,13},{13,1},{2,6},{6,10},{... | collective-permute-start | bytes 1572872 | tf_op jit(solution)/shard_map/ppermute | solution.py:54
  329.5 66.8 %collective-permute-start.13 = (bf16[128,2048]{1,0:T(8,128)(2,1)}, bf16[128,2048]{1,0:T(8,128)(2,1)}, u32[]{:S(2)}, u32[]{:S(2)}) collective-permute-start(bf16[128,2048]{1,0:T(8,128)(2,1)} %fusion.76), channel_id=1, source_target_pairs={{0,12},{4,0},{8,4},{12,8},{1,13},{5,1},{9,5},{13,9},{2,14},{6,2},{... | collective-permute-start | bytes 1572872 | tf_op jit(solution)/shard_map/ppermute | solution.py:54
  342.3 63.5 %collective-permute-start.12 = (bf16[128,2048]{1,0:T(8,128)(2,1)}, bf16[128,2048]{1,0:T(8,128)(2,1)}, u32[]{:S(2)}, u32[]{:S(2)}) collective-permute-start(bf16[128,2048]{1,0:T(8,128)(2,1)} %fusion.76), channel_id=1, source_target_pairs={{0,8},{4,12},{8,0},{12,4},{1,9},{5,13},{9,1},{13,5},{2,10},{6,14},... | collective-permute-start | bytes 1572872 | tf_op jit(solution)/shard_map/ppermute | solution.py:54
  342.8 64.7 %collective-permute-start.11 = (bf16[128,2048]{1,0:T(8,128)(2,1)}, bf16[128,2048]{1,0:T(8,128)(2,1)}, u32[]{:S(2)}, u32[]{:S(2)}) collective-permute-start(bf16[128,2048]{1,0:T(8,128)(2,1)} %fusion.76), channel_id=1, source_target_pairs={{0,4},{4,8},{8,12},{12,0},{1,5},{5,9},{9,13},{13,1},{2,6},{6,10},{... | collective-permute-start | bytes 1572872 | tf_op jit(solution)/shard_map/ppermute | solution.py:54
  394.7 72.2 %collective-permute-start.17 = (bf16[3,1024,512]{2,1,0:T(8,128)(2,1)}, bf16[3,1024,512]{2,1,0:T(8,128)(2,1)}, u32[]{:S(2)}, u32[]{:S(2)}) collective-permute-start(bf16[3,1024,512]{2,1,0:T(8,128)(2,1)} %bitcast.499), channel_id=1, source_target_pairs={{0,18},{1,19},{2,16},{3,17},{16,2},{17,3},{18,0},{19,1},{4,22},{5,... | collective-permute-start | bytes 9437192 | tf_op jit(solution)/shard_map/ppermute | solution.py:65
  396.3 137.5 %collective-permute-start.16 = (bf16[3,1024,512]{2,1,0:T(8,128)(2,1)}, bf16[3,1024,512]{2,1,0:T(8,128)(2,1)}, u32[]{:S(2)}, u32[]{:S(2)}) collective-permute-start(bf16[3,1024,512]{2,1,0:T(8,128)(2,1)} %bitcast.500), channel_id=1, source_target_pairs={{0,2},{1,3},{2,0},{3,1},{16,18},{17,19},{18,16},{19,17},{4,6},{5,7... | collective-permute-start | bytes 9437192 | tf_op jit(solution)/shard_map/ppermute | solution.py:65
  405.8 128.1 %collective-permute-start.15 = (bf16[3,1024,512]{2,1,0:T(8,128)(2,1)}, bf16[3,1024,512]{2,1,0:T(8,128)(2,1)}, u32[]{:S(2)}, u32[]{:S(2)}) collective-permute-start(bf16[3,1024,512]{2,1,0:T(8,128)(2,1)} %bitcast.501), channel_id=1, source_target_pairs={{0,16},{1,17},{2,18},{3,19},{16,0},{17,1},{18,2},{19,3},{4,20},{5,... | collective-permute-start | bytes 9437192 | tf_op jit(solution)/shard_map/ppermute | solution.py:65
  648.2 77.9 %collective-permute-start.20 = (bf16[128,2048]{1,0:T(8,128)(2,1)S(1)}, bf16[128,2048]{1,0:T(8,128)(2,1)S(1)}, u32[]{:S(2)}, u32[]{:S(2)}) collective-permute-start(bf16[128,2048]{1,0:T(8,128)(2,1)S(1)} %get-tuple-element.84), channel_id=1, source_target_pairs={{0,8},{4,12},{8,0},{12,4},{1,9},{5,13},{9,1},{13,5},{2,10},{6,14},... | collective-permute-start | bytes 1572872 | tf_op jit(solution)/shard_map/ppermute | solution.py:54
  659.7 66.4 %collective-permute-start.19 = (bf16[128,2048]{1,0:T(8,128)(2,1)S(1)}, bf16[128,2048]{1,0:T(8,128)(2,1)S(1)}, u32[]{:S(2)}, u32[]{:S(2)}) collective-permute-start(bf16[128,2048]{1,0:T(8,128)(2,1)S(1)} %get-tuple-element.82), channel_id=1, source_target_pairs={{0,12},{4,0},{8,4},{12,8},{1,13},{5,1},{9,5},{13,9},{2,14},{6,2},{... | collective-permute-start | bytes 1572872 | tf_op jit(solution)/shard_map/ppermute | solution.py:54
  795.9 72.2 %collective-permute-start.43 = (bf16[3,1024,512]{2,1,0:T(8,128)(2,1)}, bf16[3,1024,512]{2,1,0:T(8,128)(2,1)}, u32[]{:S(2)}, u32[]{:S(2)}) collective-permute-start(bf16[3,1024,512]{2,1,0:T(8,128)(2,1)} %get-tuple-element.51), channel_id=1, source_target_pairs={{0,18},{1,19},{2,16},{3,17},{16,2},{17,3},{18,0},{19,1},{4,22},{5,... | collective-permute-start | bytes 9437192 | tf_op jit(solution)/shard_map/ppermute | solution.py:65
  797.6 148.7 %collective-permute-start.42 = (bf16[3,1024,512]{2,1,0:T(8,128)(2,1)}, bf16[3,1024,512]{2,1,0:T(8,128)(2,1)}, u32[]{:S(2)}, u32[]{:S(2)}) collective-permute-start(bf16[3,1024,512]{2,1,0:T(8,128)(2,1)} %get-tuple-element.52), channel_id=1, source_target_pairs={{0,2},{1,3},{2,0},{3,1},{16,18},{17,19},{18,16},{19,17},{4,6},{5,7... | collective-permute-start | bytes 9437192 | tf_op jit(solution)/shard_map/ppermute | solution.py:65
  798.9 147.4 %collective-permute-start.41 = (bf16[3,1024,512]{2,1,0:T(8,128)(2,1)}, bf16[3,1024,512]{2,1,0:T(8,128)(2,1)}, u32[]{:S(2)}, u32[]{:S(2)}) collective-permute-start(bf16[3,1024,512]{2,1,0:T(8,128)(2,1)} %get-tuple-element.50), channel_id=1, source_target_pairs={{0,16},{1,17},{2,18},{3,19},{16,0},{17,1},{18,2},{19,3},{4,20},{5,... | collective-permute-start | bytes 9437192 | tf_op jit(solution)/shard_map/ppermute | solution.py:65
  845.0 135.0 %collective-permute-start.34 = (bf16[4,128,2048]{2,1,0:T(8,128)(2,1)}, bf16[4,128,2048]{2,1,0:T(8,128)(2,1)}, u32[]{:S(2)}, u32[]{:S(2)}) collective-permute-start(bf16[4,128,2048]{2,1,0:T(8,128)(2,1)} %slice_bitcast_fusion.14), channel_id=1, source_target_pairs={{0,1},{1,0},{2,3},{3,2},{4,5},{5,4},{6,7},{7,6},{8,9},{9,8},{10,11... | collective-permute-start | bytes 6291464 | tf_op jit(solution)/shard_map/ppermute | solution.py:57
  958.2 142.7 %all-to-all-start.3 = ((bf16[3,1024,512]{2,0,1:T(4,128)(2,1)}), bf16[3,1024,512]{2,0,1:T(4,128)(2,1)}, u32[]{:S(2)}, u32[]{:S(2)}) async-start(bf16[3,1024,512]{2,0,1:T(4,128)(2,1)} %copy.377), calls=%async_computation.3 | async-start | bytes 8388608 | tf_op jit(solution)/shard_map/all_to_all | solution.py:100
  963.1 263.3 %all-gather.5.cloned.1.call-start = ((), (), s32[]{:S(2)}) async-start(), calls=%async_computation.5 | async-start | bytes 5242880 | tf_op jit(solution)/shard_map/all_gather | solution.py:242
  983.4 64.0 %collective-permute-start.37 = (bf16[128,2048]{1,0:T(8,128)(2,1)S(1)}, bf16[128,2048]{1,0:T(8,128)(2,1)S(1)}, u32[]{:S(2)}, u32[]{:S(2)}) collective-permute-start(bf16[128,2048]{1,0:T(8,128)(2,1)S(1)} %get-tuple-element.71), channel_id=1, source_target_pairs={{0,4},{4,8},{8,12},{12,0},{1,5},{5,9},{9,13},{13,1},{2,6},{6,10},{... | collective-permute-start | bytes 1572872 | tf_op jit(solution)/shard_map/ppermute | solution.py:54
  985.3 105.9 %collective-permute-start.36 = (bf16[128,2048]{1,0:T(8,128)(2,1)S(1)}, bf16[128,2048]{1,0:T(8,128)(2,1)S(1)}, u32[]{:S(2)}, u32[]{:S(2)}) collective-permute-start(bf16[128,2048]{1,0:T(8,128)(2,1)S(1)} %get-tuple-element.72), channel_id=1, source_target_pairs={{0,8},{4,12},{8,0},{12,4},{1,9},{5,13},{9,1},{13,5},{2,10},{6,14},... | collective-permute-start | bytes 1572872 | tf_op jit(solution)/shard_map/ppermute | solution.py:54
  987.7 103.6 %collective-permute-start.35 = (bf16[128,2048]{1,0:T(8,128)(2,1)S(1)}, bf16[128,2048]{1,0:T(8,128)(2,1)S(1)}, u32[]{:S(2)}, u32[]{:S(2)}) collective-permute-start(bf16[128,2048]{1,0:T(8,128)(2,1)S(1)} %get-tuple-element.70), channel_id=1, source_target_pairs={{0,12},{4,0},{8,4},{12,8},{1,13},{5,1},{9,5},{13,9},{2,14},{6,2},{... | collective-permute-start | bytes 1572872 | tf_op jit(solution)/shard_map/ppermute | solution.py:54
  991.9 104.8 %collective-permute-start.40 = (bf16[4,1024,128]{2,1,0:T(8,128)(2,1)}, bf16[4,1024,128]{2,1,0:T(8,128)(2,1)}, u32[]{:S(2)}, u32[]{:S(2)}) collective-permute-start(bf16[4,1024,128]{2,1,0:T(8,128)(2,1)} %get-tuple-element.65), channel_id=1, source_target_pairs={{0,18},{1,19},{2,16},{3,17},{16,2},{17,3},{18,0},{19,1},{4,22},{5,... | collective-permute-start | bytes 3145736 | tf_op jit(solution)/shard_map/ppermute | solution.py:65
  993.6 103.2 %collective-permute-start.39 = (bf16[4,1024,128]{2,1,0:T(8,128)(2,1)}, bf16[4,1024,128]{2,1,0:T(8,128)(2,1)}, u32[]{:S(2)}, u32[]{:S(2)}) collective-permute-start(bf16[4,1024,128]{2,1,0:T(8,128)(2,1)} %get-tuple-element.66), channel_id=1, source_target_pairs={{0,2},{1,3},{2,0},{3,1},{16,18},{17,19},{18,16},{19,17},{4,6},{5,7... | collective-permute-start | bytes 3145736 | tf_op jit(solution)/shard_map/ppermute | solution.py:65
  1047.4 49.4 %collective-permute-start.38 = (bf16[4,1024,128]{2,1,0:T(8,128)(2,1)}, bf16[4,1024,128]{2,1,0:T(8,128)(2,1)}, u32[]{:S(2)}, u32[]{:S(2)}) collective-permute-start(bf16[4,1024,128]{2,1,0:T(8,128)(2,1)} %get-tuple-element.64), channel_id=1, source_target_pairs={{0,16},{1,17},{2,18},{3,19},{16,0},{17,1},{18,2},{19,3},{4,20},{5,... | collective-permute-start | bytes 3145736 | tf_op jit(solution)/shard_map/ppermute | solution.py:65
  1100.9 51.1 %all-to-all-start.2 = ((bf16[4,1024,128]{2,0,1:T(4,128)(2,1)}), bf16[4,1024,128]{2,0,1:T(4,128)(2,1)S(1)}, u32[]{:S(2)}, u32[]{:S(2)}) async-start(bf16[4,1024,128]{2,0,1:T(4,128)(2,1)} %copy.371), calls=%async_computation.2 | async-start | bytes 2097152 | tf_op jit(solution)/shard_map/all_to_all | solution.py:100
  (97 other events, 2470.4 us)
Sparse Core Ops, SparseCore 0:
  812.9 78.6 all-gather.2
  1093.7 43.1 all-gather.4
where the time goes:
time: 1250 us; the launch traced here: 1240 us
  waiting for transfers between devices  598 us (48%)
  starting transfers between devices  175 us (14%)
  local copies, waits for them, and re-layouts  154 us (12%)
  other arithmetic  139 us (11%)
  matrix products  114 us (9%)
  blocking collectives  40.1 us (3%)
  between operations  19.1 us (2%)
    ppermute x24, waiting for transfers between devices, by_ctx(): lax.ppermute(block, 'ctx', [(i, (i + shift) % n_c) for i in range(n_c)])  370 us
    ppermute x12, waiting for transfers between devices, by_pack(): return lax.ppermute(block, ('fsdp', 'tp'), pairs)  222 us
    ppermute x24, starting transfers between devices, by_ctx(): lax.ppermute(block, 'ctx', [(i, (i + shift) % n_c) for i in range(n_c)])  125 us
    dot_general x21, matrix products, dot(): lax.dot_general(left, right, (dims, ((), ())), preferred_element_type=F32)  95.9 us
    psum x1, blocking collectives, shards(): lax.psum(jnp.sum(att_total * att_total) + jnp.sum(ff_total * ff_total), (...  40.1 us
    dot_general x6, local copies, waits for them, and re-layouts, dot(): lax.dot_general(left, right, (dims, ((), ())), preferred_element_type=F32)  35.6 us
    unnamed x169, local copies, waits for them, and re-layouts  31.6 us
    all_to_all x2, starting transfers between devices, scatter_grad(): return lax.all_to_all(total.astype(BF), 'ctx', 1, 2, tiled=True).astype(F32)  25.3 us
  transfers between devices with their start and end apart: 50, of which 22 were waited for; matrix products, arithmetic and copies ran while one was open for 22% of the time, Pallas kernels for 0%

commit v1 on v0

--- a/solution.py
+++ b/solution.py
@@ -16,6 +16,40 @@
 F32 = jnp.float32
 
 
+def bring_stops_all(vals, k_dim, array_in):
+    m_next = vals.shape
+    w_next = vals.reshape(
+        *m_next[:k_dim], array_in, m_next[k_dim] // array_in, *m_next[k_dim + 1 :]
+    )
+    o_now = jnp.moveaxis(w_next, k_dim, 0)
+    return o_now
+
+
+def group_the_sizes(field, dim_no):
+    met_up = list(field.shape[1:])
+    met_up[dim_no] *= field.shape[0]
+    row_out = jnp.moveaxis(field, 0, dim_no).reshape(met_up)
+    return row_out
+
+
+def extend_frames(local_block, device_axis, a0, base_x):
+    x_now, heard = (lax.axis_size(device_axis), lax.axis_index(device_axis))
+    moved = bring_stops_all(local_block, a0, x_now)
+    dev_i = 1
+    series = [moved[heard]]
+    while dev_i < x_now:
+        back = moved[heard ^ dev_i]
+        series.append(
+            lax.ppermute(
+                back, axis_name=device_axis, perm=[(num, num ^ dev_i) for num in range(x_now)]
+            )
+        )
+        dev_i += 1
+    moved = jnp.stack(series)[heard ^ jnp.arange(x_now)]
+    a_next = group_the_sizes(moved, base_x)
+    return a_next
+
+
 def mean_spread(values):
     centre = values - jnp.mean(values, axis=-1, keepdims=True)
     spread = jnp.mean(centre * centre, axis=-1, keepdims=True)
@@ -80,7 +114,7 @@
         return total
 
     def gather_weight(shard):
-        swapped = lax.all_to_all(shard.astype(BF), "ctx", 2, 1, tiled=True)
+        swapped = extend_frames(shard.astype(BF), "ctx", 2, 1)
         columns = []
         for other in range(2):
             parts = [

time: 1250 us -> 1190 us (0.952)
  starting transfers between devices: 175 us -> 133 us
  waiting for transfers between devices: 598 us -> 566 us
  local copies, waits for them, and re-layouts: 154 us -> 171 us
    ppermute x24, waiting for transfers between devices: 370 us -> 293 us  [by_ctx(): lax.ppermute(block, 'ctx', [(i, (i + shift) % n_c) for i in range(n_c)])]
    ppermute x24, starting transfers between devices: 125 us -> 50.3 us  [by_ctx(): lax.ppermute(block, 'ctx', [(i, (i + shift) % n_c) for i in range(n_c)])]
    ppermute x0 -> x6, waiting for transfers between devices: none -> 54.8 us  [extend_frames(): lax.ppermute(back, axis_name=device_axis, perm=[(num, num ^ dev_i) for nu...]
    ppermute x0 -> x6, starting transfers between devices: none -> 41.6 us  [extend_frames(): lax.ppermute(back, axis_name=device_axis, perm=[(num, num ^ dev_i) for nu...]
    unnamed x169 -> x192, local copies, waits for them, and re-layouts: 31.6 us -> 41 us
    another operation x2 -> x10, local copies, waits for them, and re-layouts: 19 us -> 26 us
    dot_general x6 -> x10, local copies, waits for them, and re-layouts: 35.6 us -> 41.6 us  [dot(): lax.dot_general(left, right, (dims, ((), ())), preferred_element_type=F32)]
  transfers between devices with their start and end apart: 50 -> 54, of which waited for: 22 -> 23; matrix products, arithmetic and copies ran while one was open for 22% -> 25% of each run, Pallas kernels for 0% -> 0%
where the time goes in v1:
time: 1190 us
  waiting for transfers between devices  566 us (48%)
  local copies, waits for them, and re-layouts  171 us (14%)
  other arithmetic  140 us (12%)
  starting transfers between devices  133 us (11%)
  matrix products  119 us (10%)
  blocking collectives  40.1 us (3%)
  between operations  19.2 us (2%)
    ppermute x24, waiting for transfers between devices, by_ctx(): lax.ppermute(block, 'ctx', [(i, (i + shift) % n_c) for i in range(n_c)])  293 us
    ppermute x12, waiting for transfers between devices, by_pack(): return lax.ppermute(block, ('fsdp', 'tp'), pairs)  218 us
    dot_general x21, matrix products, dot(): lax.dot_general(left, right, (dims, ((), ())), preferred_element_type=F32)  102 us
    ppermute x6, waiting for transfers between devices, extend_frames(): lax.ppermute(back, axis_name=device_axis, perm=[(num, num ^ dev_i) for nu...  54.8 us
    ppermute x24, starting transfers between devices, by_ctx(): lax.ppermute(block, 'ctx', [(i, (i + shift) % n_c) for i in range(n_c)])  50.3 us
    dot_general x10, local copies, waits for them, and re-layouts, dot(): lax.dot_general(left, right, (dims, ((), ())), preferred_element_type=F32)  41.6 us
    ppermute x6, starting transfers between devices, extend_frames(): lax.ppermute(back, axis_name=device_axis, perm=[(num, num ^ dev_i) for nu...  41.6 us
    unnamed x192, local copies, waits for them, and re-layouts  41 us
  transfers between devices with their start and end apart: 54, of which 23 were waited for; matrix products, arithmetic and copies ran while one was open for 25% of the time, Pallas kernels for 0%

profile of v1, /device:TPU:0, one launch (start us, length us, event | category | flops | bytes accessed | tf_op | source)
XLA Modules:
  0.0 1186.6 jit_solution(6641780499520910830)
XLA Ops:
  28.0 33.1 %collective-permute-start.4 = (bf16[4,256,128]{2,1,0:T(8,128)(2,1)S(1)}, bf16[4,256,128]{2,1,0:T(8,128)(2,1)S(1)}, u32[]{:S(2)}, u32[]{:S(2)}) collective-permute-start(bf16[4,256,128]{2,1,0:T(8,128)(2,1)S(1)} %bitcast.562), channel_id=1, source_target_pairs={{0,4},{4,0},{8,12},{12,8},{1,5},{5,1},{9,13},{13,9},{2,6},{6,2},{1... | collective-permute-start | bytes 786440 | tf_op jit(solution)/shard_map/ppermute | solution.py:43
  61.1 11.8 collective-permute-done.1
  91.4 19.5 %collective-permute-done.9 = bf16[4,1024,128]{2,1,0:T(8,128)(2,1)S(1)} collective-permute-done((bf16[4,1024,128]{2,1,0:T(8,128)(2,1)S(1)}, bf16[4,1024,128]{2,1,0:T(8,128)(2,1)S(1)}, u32[]{:S(2)}, u32[]{:S(2)}) %collective-permute-start.9) | collective-permute-done | bytes 1048608 | tf_op jit(solution)/shard_map/ppermute | solution.py:99
  110.9 20.5 %collective-permute-done.8 = bf16[4,1024,128]{2,1,0:T(8,128)(2,1)} collective-permute-done((bf16[4,1024,128]{2,1,0:T(8,128)(2,1)S(1)}, bf16[4,1024,128]{2,1,0:T(8,128)(2,1)}, u32[]{:S(2)}, u32[]{:S(2)}) %collective-permute-start.8) | collective-permute-done | bytes 1048608 | tf_op jit(solution)/shard_map/ppermute | solution.py:99
  150.6 7.4 fusion.135
  202.4 52.3 %collective-permute-done.29 = bf16[128,2048]{1,0:T(8,128)(2,1)} collective-permute-done((bf16[128,2048]{1,0:T(8,128)(2,1)}, bf16[128,2048]{1,0:T(8,128)(2,1)}, u32[]{:S(2)}, u32[]{:S(2)}) %collective-permute-start.29) | collective-permute-done | bytes 524320 | tf_op jit(solution)/shard_map/ppermute | solution.py:88
  262.3 48.6 %collective-permute-done.19 = bf16[3,256,512]{2,1,0:T(8,128)(2,1)S(1)} collective-permute-done((bf16[3,256,512]{2,1,0:T(8,128)(2,1)}, bf16[3,256,512]{2,1,0:T(8,128)(2,1)S(1)}, u32[]{:S(2)}, u32[]{:S(2)}) %collective-permute-start.19) | collective-permute-done | bytes 786464 | tf_op jit(solution)/shard_map/ppermute | solution.py:43
  325.4 7.5 collective-permute-done.11
  340.9 12.4 %collective-permute-done.16 = bf16[128,2048]{1,0:T(8,128)(2,1)S(1)} collective-permute-done((bf16[128,2048]{1,0:T(8,128)(2,1)S(1)}, bf16[128,2048]{1,0:T(8,128)(2,1)S(1)}, u32[]{:S(2)}, u32[]{:S(2)}) %collective-permute-start.16) | collective-permute-done | bytes 524320 | tf_op jit(solution)/shard_map/ppermute | solution.py:88
  358.5 8.2 reshape.608
  366.7 11.2 copy.317
  394.0 67.0 %collective-permute-done.22 = bf16[3,1024,512]{2,1,0:T(8,128)(2,1)} collective-permute-done((bf16[3,1024,512]{2,1,0:T(8,128)(2,1)}, bf16[3,1024,512]{2,1,0:T(8,128)(2,1)}, u32[]{:S(2)}, u32[]{:S(2)}) %collective-permute-start.22) | collective-permute-done | bytes 3145760 | tf_op jit(solution)/shard_map/ppermute | solution.py:99
  461.0 14.6 %maximum_maximum_fusion = bf16[3,2048,1024]{2,1,0:T(8,128)(2,1)S(1)} fusion(bf16[3,1024,512]{2,1,0:T(8,128)(2,1)} %collective-permute-done.23, bf16[3,1024,512]{2,1,0:T(8,128)(2,1)} %collective-permute-done.22, bf16[3,1024,512]{2,1,0:T(8,128)(2,1)} %collective-permute-done.21, bf16[3,1024,512]{2,1,0:T(8,128)(2,1)} %bitcast.71), kind=kLoop, calls=%fused_computation.4 | loop fusion | flops 50331648 | bytes 25165824 | tf_op jit(solution)/shard_map/concatenate | solution.py:124
  493.6 8.1 fusion.22
  503.7 11.1 fusion.12
  525.7 9.3 convolution_convert_fusion.1
  535.0 13.9 %fusion.20 = f32[1024,2048]{1,0:T(8,128)} fusion(bf16[3,2048,1024]{2,1,0:T(8,128)(2,1)} %copy-done.14, f32[1024,1024]{1,0:T(8,128)S(1)} %copy-done.35, f32[1024,1024]{1,0:T(8,128)S(1)} %copy-done.31, f32[1024,1024]{1,0:T(8,128)} %copy.273), kind=kOutput, calls=%fused_computation.66 | convolution fusion | flops 4305453056 | bytes 25165824 | tf_op jit(solution)/shard_map/dot_general | solution.py:69
  549.0 11.6 add_convert_fusion.1
  595.3 9.4 collective-permute-done.35
  607.9 19.3 %collective-permute-done.34 = bf16[128,2048]{1,0:T(8,128)(2,1)} collective-permute-done((bf16[128,2048]{1,0:T(8,128)(2,1)}, bf16[128,2048]{1,0:T(8,128)(2,1)}, u32[]{:S(2)}, u32[]{:S(2)}) %collective-permute-start.34) | collective-permute-done | bytes 524320 | tf_op jit(solution)/shard_map/ppermute | solution.py:88
  629.0 9.3 collective-permute-done.27
  638.3 33.1 %collective-permute-done.26 = bf16[128,2048]{1,0:T(8,128)(2,1)S(1)} collective-permute-done((bf16[128,2048]{1,0:T(8,128)(2,1)S(1)}, bf16[128,2048]{1,0:T(8,128)(2,1)S(1)}, u32[]{:S(2)}, u32[]{:S(2)}) %collective-permute-start.26) | collective-permute-done | bytes 524320 | tf_op jit(solution)/shard_map/ppermute | solution.py:88
  672.2 10.9 collective-permute-start.38
  685.5 7.5 convolution_bitcast_fusion
  696.1 34.9 %collective-permute-done.37 = bf16[128,2048]{1,0:T(8,128)(2,1)S(1)} collective-permute-done((bf16[128,2048]{1,0:T(8,128)(2,1)S(1)}, bf16[128,2048]{1,0:T(8,128)(2,1)S(1)}, u32[]{:S(2)}, u32[]{:S(2)}) %collective-permute-start.37) | collective-permute-done | bytes 524320 | tf_op jit(solution)/shard_map/ppermute | solution.py:88
  746.2 12.4 %pad_maximum_fusion = f32[3,2,1024,2,512]{4,2,3,1,0:T(8,128)} fusion(f32[1,2,1024,2,512]{4,2,3,1,0:T(8,128)} %convolution_bitcast_fusion, f32[1,2,1024,2,512]{4,2,3,1,0:T(8,128)S(1)} %convolution_bitcast_fusion.1, f32[1,2,1024,2,512]{4,2,3,1,0:T(8,128)S(1)} %convolution_bitcast_fusion.2), kind=kLoop, calls=%fused_computation.3 | loop fusion | flops 12582912 | bytes 50331648 | tf_op jit(solution)/shard_map/stack | solution.py:247
  787.5 27.3 %collective-permute-done.49 = bf16[3,1024,512]{2,1,0:T(8,128)(2,1)} collective-permute-done((bf16[3,1024,512]{2,1,0:T(8,128)(2,1)}, bf16[3,1024,512]{2,1,0:T(8,128)(2,1)}, u32[]{:S(2)}, u32[]{:S(2)}) %collective-permute-start.49) | collective-permute-done | bytes 3145760 | tf_op jit(solution)/shard_map/ppermute | solution.py:99
  814.9 78.2 %collective-permute-done.48 = bf16[3,1024,512]{2,1,0:T(8,128)(2,1)} collective-permute-done((bf16[3,1024,512]{2,1,0:T(8,128)(2,1)}, bf16[3,1024,512]{2,1,0:T(8,128)(2,1)}, u32[]{:S(2)}, u32[]{:S(2)}) %collective-permute-start.48) | collective-permute-done | bytes 3145760 | tf_op jit(solution)/shard_map/ppermute | solution.py:99
  941.7 52.7 %collective-permute-done.43 = bf16[128,2048]{1,0:T(8,128)(2,1)S(1)} collective-permute-done((bf16[128,2048]{1,0:T(8,128)(2,1)S(1)}, bf16[128,2048]{1,0:T(8,128)(2,1)S(1)}, u32[]{:S(2)}, u32[]{:S(2)}) %collective-permute-start.43) | collective-permute-done | bytes 524320 | tf_op jit(solution)/shard_map/ppermute | solution.py:88
  995.9 42.4 %collective-permute-done.42 = bf16[128,2048]{1,0:T(8,128)(2,1)S(1)} collective-permute-done((bf16[128,2048]{1,0:T(8,128)(2,1)S(1)}, bf16[128,2048]{1,0:T(8,128)(2,1)S(1)}, u32[]{:S(2)}, u32[]{:S(2)}) %collective-permute-start.42) | collective-permute-done | bytes 524320 | tf_op jit(solution)/shard_map/ppermute | solution.py:88
  1047.9 20.4 %all-to-all-start = ((bf16[4,1024,128]{2,0,1:T(4,128)(2,1)}), bf16[4,1024,128]{2,0,1:T(4,128)(2,1)S(1)}, u32[]{:S(2)}, u32[]{:S(2)}) async-start(bf16[4,1024,128]{2,0,1:T(4,128)(2,1)} %copy.298), calls=%async_computation | async-start | bytes 2097152 | tf_op jit(solution)/shard_map/all_to_all | solution.py:134
  1105.8 40.1 %psum.7 = f32[]{:T(128)} all-reduce(f32[]{:T(128)S(6)} %add.457), channel_id=1, replica_groups=mesh['fsdp'=2,'ctx'=4,'tp'=4] {'fsdp','ctx','tp'}, use_global_device_ids=true, to_apply=%region_15.16 | all-reduce | flops 1 | bytes 8 | tf_op jit(solution)/shard_map/psum | solution.py:282
  (423 shorter events, 401.5 us)
Async XLA Ops:
  7.2 1061.1 %all-gather.3.cloned.1.call-start = ((), (), s32[]{:S(2)}) async-start(), calls=%async_computation.2 | async-start | bytes 2621440 | tf_op jit(solution)/shard_map/all_gather | solution.py:246
  15.3 57.5 %collective-permute-start.1 = (bf16[128,2048]{1,0:T(8,128)(2,1)}, bf16[128,2048]{1,0:T(8,128)(2,1)}, u32[]{:S(2)}, u32[]{:S(2)}) collective-permute-start(bf16[128,2048]{1,0:T(8,128)(2,1)} %fusion.49), channel_id=1, source_target_pairs={{0,8},{4,12},{8,0},{12,4},{1,9},{5,13},{9,1},{13,5},{2,10},{6,14},... | collective-permute-start | bytes 1572872 | tf_op jit(solution)/shard_map/ppermute | solution.py:88
  15.3 57.5 %collective-permute-start = (bf16[128,2048]{1,0:T(8,128)(2,1)}, bf16[128,2048]{1,0:T(8,128)(2,1)}, u32[]{:S(2)}, u32[]{:S(2)}) collective-permute-start(bf16[128,2048]{1,0:T(8,128)(2,1)} %fusion.49), channel_id=1, source_target_pairs={{0,4},{4,8},{8,12},{12,0},{1,5},{5,9},{9,13},{13,1},{2,6},{6,10},{... | collective-permute-start | bytes 1572872 | tf_op jit(solution)/shard_map/ppermute | solution.py:88
  18.1 58.5 %collective-permute-start.6 = (bf16[4,256,128]{2,1,0:T(8,128)(2,1)S(1)}, bf16[4,256,128]{2,1,0:T(8,128)(2,1)S(1)}, u32[]{:S(2)}, u32[]{:S(2)}) collective-permute-start(bf16[4,256,128]{2,1,0:T(8,128)(2,1)S(1)} %bitcast.560), channel_id=1, source_target_pairs={{0,12},{4,8},{8,4},{12,0},{1,13},{5,9},{9,5},{13,1},{2,14},{6,10},... | collective-permute-start | bytes 786440 | tf_op jit(solution)/shard_map/ppermute | solution.py:43
  21.2 61.7 %collective-permute-start.5 = (bf16[4,256,128]{2,1,0:T(8,128)(2,1)S(1)}, bf16[4,256,128]{2,1,0:T(8,128)(2,1)S(1)}, u32[]{:S(2)}, u32[]{:S(2)}) collective-permute-start(bf16[4,256,128]{2,1,0:T(8,128)(2,1)S(1)} %bitcast.561), channel_id=1, source_target_pairs={{0,8},{4,12},{8,0},{12,4},{1,9},{5,13},{9,1},{13,5},{2,10},{6,14},... | collective-permute-start | bytes 786440 | tf_op jit(solution)/shard_map/ppermute | solution.py:43
  28.0 54.8 %collective-permute-start.4 = (bf16[4,256,128]{2,1,0:T(8,128)(2,1)S(1)}, bf16[4,256,128]{2,1,0:T(8,128)(2,1)S(1)}, u32[]{:S(2)}, u32[]{:S(2)}) collective-permute-start(bf16[4,256,128]{2,1,0:T(8,128)(2,1)S(1)} %bitcast.562), channel_id=1, source_target_pairs={{0,4},{4,0},{8,12},{12,8},{1,5},{5,1},{9,13},{13,9},{2,6},{6,2},{1... | collective-permute-start | bytes 786440 | tf_op jit(solution)/shard_map/ppermute | solution.py:43
  76.6 65.0 %collective-permute-start.3 = (bf16[4,128,2048]{2,1,0:T(8,128)(2,1)}, bf16[4,128,2048]{2,1,0:T(8,128)(2,1)}, u32[]{:S(2)}, u32[]{:S(2)}) collective-permute-start(bf16[4,128,2048]{2,1,0:T(8,128)(2,1)} %get-tuple-element.95), channel_id=1, source_target_pairs={{0,1},{1,0},{2,3},{3,2},{4,5},{5,4},{6,7},{7,6},{8,9},{9,8},{10,11... | collective-permute-start | bytes 6291464 | tf_op jit(solution)/shard_map/ppermute | solution.py:91
  175.6 79.1 %collective-permute-start.29 = (bf16[128,2048]{1,0:T(8,128)(2,1)}, bf16[128,2048]{1,0:T(8,128)(2,1)}, u32[]{:S(2)}, u32[]{:S(2)}) collective-permute-start(bf16[128,2048]{1,0:T(8,128)(2,1)} %get-tuple-element.116), channel_id=1, source_target_pairs={{0,8},{4,12},{8,0},{12,4},{1,9},{5,13},{9,1},{13,5},{2,10},{6,14},... | collective-permute-start | bytes 1572872 | tf_op jit(solution)/shard_map/ppermute | solution.py:88
  175.6 79.1 %collective-permute-start.28 = (bf16[128,2048]{1,0:T(8,128)(2,1)}, bf16[128,2048]{1,0:T(8,128)(2,1)}, u32[]{:S(2)}, u32[]{:S(2)}) collective-permute-start(bf16[128,2048]{1,0:T(8,128)(2,1)} %get-tuple-element.116), channel_id=1, source_target_pairs={{0,4},{4,8},{8,12},{12,0},{1,5},{5,9},{9,13},{13,1},{2,6},{6,10},{... | collective-permute-start | bytes 1572872 | tf_op jit(solution)/shard_map/ppermute | solution.py:88
  187.8 70.4 %collective-permute-start.20 = (bf16[3,256,512]{2,1,0:T(8,128)(2,1)}, bf16[3,256,512]{2,1,0:T(8,128)(2,1)}, u32[]{:S(2)}, u32[]{:S(2)}) collective-permute-start(bf16[3,256,512]{2,1,0:T(8,128)(2,1)} %bitcast.68), channel_id=1, source_target_pairs={{0,12},{4,8},{8,4},{12,0},{1,13},{5,9},{9,5},{13,1},{2,14},{6,10},... | collective-permute-start | bytes 2359304 | tf_op jit(solution)/shard_map/ppermute | solution.py:43
  194.8 116.1 %collective-permute-start.19 = (bf16[3,256,512]{2,1,0:T(8,128)(2,1)}, bf16[3,256,512]{2,1,0:T(8,128)(2,1)S(1)}, u32[]{:S(2)}, u32[]{:S(2)}) collective-permute-start(bf16[3,256,512]{2,1,0:T(8,128)(2,1)} %bitcast.552), channel_id=1, source_target_pairs={{0,8},{4,12},{8,0},{12,4},{1,9},{5,13},{9,1},{13,5},{2,10},{6,14},... | collective-permute-start | bytes 2359304 | tf_op jit(solution)/shard_map/ppermute | solution.py:43
  196.0 114.9 %collective-permute-start.18 = (bf16[3,256,512]{2,1,0:T(8,128)(2,1)}, bf16[3,256,512]{2,1,0:T(8,128)(2,1)S(1)}, u32[]{:S(2)}, u32[]{:S(2)}) collective-permute-start(bf16[3,256,512]{2,1,0:T(8,128)(2,1)} %bitcast.551), channel_id=1, source_target_pairs={{0,4},{4,0},{8,12},{12,8},{1,5},{5,1},{9,13},{13,9},{2,6},{6,2},{1... | collective-permute-start | bytes 2359304 | tf_op jit(solution)/shard_map/ppermute | solution.py:43
  254.7 68.8 %collective-permute-start.13 = (bf16[128,2048]{1,0:T(8,128)(2,1)}, bf16[128,2048]{1,0:T(8,128)(2,1)S(1)}, u32[]{:S(2)}, u32[]{:S(2)}) collective-permute-start(bf16[128,2048]{1,0:T(8,128)(2,1)} %get-tuple-element.92), channel_id=1, source_target_pairs={{0,4},{4,8},{8,12},{12,0},{1,5},{5,9},{9,13},{13,1},{2,6},{6,10},{... | collective-permute-start | bytes 1572872 | tf_op jit(solution)/shard_map/ppermute | solution.py:88
  254.7 70.1 %collective-permute-start.12 = (bf16[128,2048]{1,0:T(8,128)(2,1)}, bf16[128,2048]{1,0:T(8,128)(2,1)S(1)}, u32[]{:S(2)}, u32[]{:S(2)}) collective-permute-start(bf16[128,2048]{1,0:T(8,128)(2,1)} %get-tuple-element.93), channel_id=1, source_target_pairs={{0,8},{4,12},{8,0},{12,4},{1,9},{5,13},{9,1},{13,5},{2,10},{6,14},... | collective-permute-start | bytes 1572872 | tf_op jit(solution)/shard_map/ppermute | solution.py:88
  258.1 74.7 %collective-permute-start.11 = (bf16[128,2048]{1,0:T(8,128)(2,1)}, bf16[128,2048]{1,0:T(8,128)(2,1)S(1)}, u32[]{:S(2)}, u32[]{:S(2)}) collective-permute-start(bf16[128,2048]{1,0:T(8,128)(2,1)} %get-tuple-element.91), channel_id=1, source_target_pairs={{0,12},{4,0},{8,4},{12,8},{1,13},{5,1},{9,5},{13,9},{2,14},{6,2},{... | collective-permute-start | bytes 1572872 | tf_op jit(solution)/shard_map/ppermute | solution.py:88
  321.9 72.2 %collective-permute-start.23 = (bf16[3,1024,512]{2,1,0:T(8,128)(2,1)}, bf16[3,1024,512]{2,1,0:T(8,128)(2,1)}, u32[]{:S(2)}, u32[]{:S(2)}) collective-permute-start(bf16[3,1024,512]{2,1,0:T(8,128)(2,1)} %bitcast.71), channel_id=1, source_target_pairs={{0,18},{1,19},{2,16},{3,17},{16,2},{17,3},{18,0},{19,1},{4,22},{5,... | collective-permute-start | bytes 9437192 | tf_op jit(solution)/shard_map/ppermute | solution.py:99
  323.5 137.5 %collective-permute-start.22 = (bf16[3,1024,512]{2,1,0:T(8,128)(2,1)}, bf16[3,1024,512]{2,1,0:T(8,128)(2,1)}, u32[]{:S(2)}, u32[]{:S(2)}) collective-permute-start(bf16[3,1024,512]{2,1,0:T(8,128)(2,1)} %bitcast.71), channel_id=1, source_target_pairs={{0,2},{1,3},{2,0},{3,1},{16,18},{17,19},{18,16},{19,17},{4,6},{5,7... | collective-permute-start | bytes 9437192 | tf_op jit(solution)/shard_map/ppermute | solution.py:99
  324.8 136.2 %collective-permute-start.21 = (bf16[3,1024,512]{2,1,0:T(8,128)(2,1)}, bf16[3,1024,512]{2,1,0:T(8,128)(2,1)}, u32[]{:S(2)}, u32[]{:S(2)}) collective-permute-start(bf16[3,1024,512]{2,1,0:T(8,128)(2,1)} %bitcast.71), channel_id=1, source_target_pairs={{0,16},{1,17},{2,18},{3,19},{16,0},{17,1},{18,2},{19,3},{4,20},{5,... | collective-permute-start | bytes 9437192 | tf_op jit(solution)/shard_map/ppermute | solution.py:99
  388.6 103.0 %collective-permute-start.17 = (bf16[4,128,2048]{2,1,0:T(8,128)(2,1)}, bf16[4,128,2048]{2,1,0:T(8,128)(2,1)}, u32[]{:S(2)}, u32[]{:S(2)}) collective-permute-start(bf16[4,128,2048]{2,1,0:T(8,128)(2,1)} %get-tuple-element.90), channel_id=1, source_target_pairs={{0,1},{1,0},{2,3},{3,2},{4,5},{5,4},{6,7},{7,6},{8,9},{9,8},{10,11... | collective-permute-start | bytes 6291464 | tf_op jit(solution)/shard_map/ppermute | solution.py:91
  595.3 76.1 %collective-permute-start.26 = (bf16[128,2048]{1,0:T(8,128)(2,1)S(1)}, bf16[128,2048]{1,0:T(8,128)(2,1)S(1)}, u32[]{:S(2)}, u32[]{:S(2)}) collective-permute-start(bf16[128,2048]{1,0:T(8,128)(2,1)S(1)} %get-tuple-element.88), channel_id=1, source_target_pairs={{0,8},{4,12},{8,0},{12,4},{1,9},{5,13},{9,1},{13,5},{2,10},{6,14},... | collective-permute-start | bytes 1572872 | tf_op jit(solution)/shard_map/ppermute | solution.py:88
  604.7 66.7 %collective-permute-start.25 = (bf16[128,2048]{1,0:T(8,128)(2,1)S(1)}, bf16[128,2048]{1,0:T(8,128)(2,1)S(1)}, u32[]{:S(2)}, u32[]{:S(2)}) collective-permute-start(bf16[128,2048]{1,0:T(8,128)(2,1)S(1)} %get-tuple-element.86), channel_id=1, source_target_pairs={{0,12},{4,0},{8,4},{12,8},{1,13},{5,1},{9,5},{13,9},{2,14},{6,2},{... | collective-permute-start | bytes 1572872 | tf_op jit(solution)/shard_map/ppermute | solution.py:88
  742.7 72.2 %collective-permute-start.49 = (bf16[3,1024,512]{2,1,0:T(8,128)(2,1)}, bf16[3,1024,512]{2,1,0:T(8,128)(2,1)}, u32[]{:S(2)}, u32[]{:S(2)}) collective-permute-start(bf16[3,1024,512]{2,1,0:T(8,128)(2,1)} %get-tuple-element.51), channel_id=1, source_target_pairs={{0,18},{1,19},{2,16},{3,17},{16,2},{17,3},{18,0},{19,1},{4,22},{5,... | collective-permute-start | bytes 9437192 | tf_op jit(solution)/shard_map/ppermute | solution.py:99
  744.4 148.7 %collective-permute-start.48 = (bf16[3,1024,512]{2,1,0:T(8,128)(2,1)}, bf16[3,1024,512]{2,1,0:T(8,128)(2,1)}, u32[]{:S(2)}, u32[]{:S(2)}) collective-permute-start(bf16[3,1024,512]{2,1,0:T(8,128)(2,1)} %get-tuple-element.52), channel_id=1, source_target_pairs={{0,2},{1,3},{2,0},{3,1},{16,18},{17,19},{18,16},{19,17},{4,6},{5,7... | collective-permute-start | bytes 9437192 | tf_op jit(solution)/shard_map/ppermute | solution.py:99
  745.7 147.4 %collective-permute-start.47 = (bf16[3,1024,512]{2,1,0:T(8,128)(2,1)}, bf16[3,1024,512]{2,1,0:T(8,128)(2,1)}, u32[]{:S(2)}, u32[]{:S(2)}) collective-permute-start(bf16[3,1024,512]{2,1,0:T(8,128)(2,1)} %get-tuple-element.50), channel_id=1, source_target_pairs={{0,16},{1,17},{2,18},{3,19},{16,0},{17,1},{18,2},{19,3},{4,20},{5,... | collective-permute-start | bytes 9437192 | tf_op jit(solution)/shard_map/ppermute | solution.py:99
  787.5 139.2 %collective-permute-start.40 = (bf16[4,128,2048]{2,1,0:T(8,128)(2,1)}, bf16[4,128,2048]{2,1,0:T(8,128)(2,1)}, u32[]{:S(2)}, u32[]{:S(2)}) collective-permute-start(bf16[4,128,2048]{2,1,0:T(8,128)(2,1)} %slice_bitcast_fusion.14), channel_id=1, source_target_pairs={{0,1},{1,0},{2,3},{3,2},{4,5},{5,4},{6,7},{7,6},{8,9},{9,8},{10,11... | collective-permute-start | bytes 6291464 | tf_op jit(solution)/shard_map/ppermute | solution.py:91
  905.2 142.6 %all-to-all-start.1 = ((bf16[3,1024,512]{2,0,1:T(4,128)(2,1)}), bf16[3,1024,512]{2,0,1:T(4,128)(2,1)}, u32[]{:S(2)}, u32[]{:S(2)}) async-start(bf16[3,1024,512]{2,0,1:T(4,128)(2,1)} %copy.304), calls=%async_computation.1 | async-start | bytes 8388608 | tf_op jit(solution)/shard_map/all_to_all | solution.py:134
  910.1 263.3 %all-gather.5.cloned.1.call-start = ((), (), s32[]{:S(2)}) async-start(), calls=%async_computation.3 | async-start | bytes 5242880 | tf_op jit(solution)/shard_map/all_gather | solution.py:276
  930.2 64.2 %collective-permute-start.43 = (bf16[128,2048]{1,0:T(8,128)(2,1)S(1)}, bf16[128,2048]{1,0:T(8,128)(2,1)S(1)}, u32[]{:S(2)}, u32[]{:S(2)}) collective-permute-start(bf16[128,2048]{1,0:T(8,128)(2,1)S(1)} %get-tuple-element.75), channel_id=1, source_target_pairs={{0,4},{4,8},{8,12},{12,0},{1,5},{5,9},{9,13},{13,1},{2,6},{6,10},{... | collective-permute-start | bytes 1572872 | tf_op jit(solution)/shard_map/ppermute | solution.py:88
  932.1 106.1 %collective-permute-start.42 = (bf16[128,2048]{1,0:T(8,128)(2,1)S(1)}, bf16[128,2048]{1,0:T(8,128)(2,1)S(1)}, u32[]{:S(2)}, u32[]{:S(2)}) collective-permute-start(bf16[128,2048]{1,0:T(8,128)(2,1)S(1)} %get-tuple-element.76), channel_id=1, source_target_pairs={{0,8},{4,12},{8,0},{12,4},{1,9},{5,13},{9,1},{13,5},{2,10},{6,14},... | collective-permute-start | bytes 1572872 | tf_op jit(solution)/shard_map/ppermute | solution.py:88
  934.5 103.8 %collective-permute-start.41 = (bf16[128,2048]{1,0:T(8,128)(2,1)S(1)}, bf16[128,2048]{1,0:T(8,128)(2,1)S(1)}, u32[]{:S(2)}, u32[]{:S(2)}) collective-permute-start(bf16[128,2048]{1,0:T(8,128)(2,1)S(1)} %get-tuple-element.74), channel_id=1, source_target_pairs={{0,12},{4,0},{8,4},{12,8},{1,13},{5,1},{9,5},{13,9},{2,14},{6,2},{... | collective-permute-start | bytes 1572872 | tf_op jit(solution)/shard_map/ppermute | solution.py:88
  938.7 105.0 %collective-permute-start.46 = (bf16[4,1024,128]{2,1,0:T(8,128)(2,1)}, bf16[4,1024,128]{2,1,0:T(8,128)(2,1)}, u32[]{:S(2)}, u32[]{:S(2)}) collective-permute-start(bf16[4,1024,128]{2,1,0:T(8,128)(2,1)} %get-tuple-element.65), channel_id=1, source_target_pairs={{0,18},{1,19},{2,16},{3,17},{16,2},{17,3},{18,0},{19,1},{4,22},{5,... | collective-permute-start | bytes 3145736 | tf_op jit(solution)/shard_map/ppermute | solution.py:99
  940.4 103.4 %collective-permute-start.45 = (bf16[4,1024,128]{2,1,0:T(8,128)(2,1)}, bf16[4,1024,128]{2,1,0:T(8,128)(2,1)}, u32[]{:S(2)}, u32[]{:S(2)}) collective-permute-start(bf16[4,1024,128]{2,1,0:T(8,128)(2,1)} %get-tuple-element.66), channel_id=1, source_target_pairs={{0,2},{1,3},{2,0},{3,1},{16,18},{17,19},{18,16},{19,17},{4,6},{5,7... | collective-permute-start | bytes 3145736 | tf_op jit(solution)/shard_map/ppermute | solution.py:99
  (111 other events, 2712.7 us)
Sparse Core Ops, SparseCore 0:
  759.6 78.7 all-gather.2
  1040.7 43.1 all-gather.4
